TPU v7x, 256 devices: a whole 4x4x8 slice. The times are simulated.
256 devices in a mesh: cuts: 8 (over x, y_lo), layer: 32 (over z, y_hi, core).
Axes of the slice: x: 4, y: 4 (y_hi: 2, y_lo: 2; y = y_hi * 2 + y_lo), z: 8, core: 2. Of those that a mesh axis runs over, the one named last changes fastest.
Arguments:
- vectors: float32 [8, 64, 64, 1024], P('cuts', None, 'layer'), may hold values from -40 to 40
- diag_blocks: bfloat16 [64, 1024, 1024], P('layer'), may hold values from -1 to 1, as said below
- couplings: bfloat16 [64, 1024, 1024], P('layer'), may hold values from -0.09375 to 0.09375
- bounds: int32 [8, 2], P('cuts'), may hold values from -128 to 160, as said below
Outputs:
- filtered: float32 [8, 64, 64, 1024], P('cuts', None, 'layer')
Inputs may be any that keep to these rules, and one draw needn't show every extreme that they name: `bounds`: column 0 holds each slice's lower end, which is -128 at slice 0 and to at most -81; column 1 holds its upper end, from 128 to 160. `diag_blocks`: each block is symmetric.
All inputs are finite; a program needn't handle non-finite values.
Results may differ from a plain program's by a relative error of at most 0.012.
Values may be sent and summed in bfloat16 or wider, within the bound.
A program may use at most 64 MiB of HBM per device.

v0:
```python
import jax
import jax.numpy as jnp
from jax import lax
from jax.sharding import PartitionSpec as P

EDGE = 16
DEG = 4


def shifted(block, axis, distance):
    devices = range(lax.axis_size(axis))
    route = [(i - distance, i) for i in devices if i - distance in devices]
    return lax.ppermute(block, axis, route)


def extended(block, sides, width):
    for axis, dim in sides:
        count = lax.axis_size(axis)
        forward = [(i, i + 1) for i in range(count - 1)]
        backward = [(target, source) for source, target in forward]
        low = lax.ppermute(
            lax.slice_in_dim(block, block.shape[dim] - width, None, axis=dim), axis, forward
        )
        high = lax.ppermute(lax.slice_in_dim(block, 0, width, axis=dim), axis, backward)
        block = jnp.concatenate([low, block, high], axis=dim)
    return block


def inner_products(first, second):
    return jnp.einsum("kn,jn->kj", first, second, precision=lax.Precision.HIGHEST)


def left_solve(factor, right_side):
    return lax.linalg.triangular_solve(factor, right_side, left_side=True, lower=True)


def per_device(vectors, diag_blocks, couplings, bounds):
    current_block = vectors[0]
    count_vec, layers, width = current_block.shape
    length_all = lax.axis_size("layer") * layers * width
    bottom = bounds[0, 0].astype(jnp.float32) / 64.0
    summit = bounds[0, 1].astype(jnp.float32) / 64.0
    centre = (bottom + summit) / 2.0
    half_width = (summit - bottom) / 2.0
    arrived_link = shifted(couplings[layers - 1 :], "layer", 1)
    links_below = jnp.concatenate([arrived_link, couplings[: layers - 1]], 0)

    def apply_operator(vectors_now):
        rounded = vectors_now.astype(jnp.bfloat16)
        padded = extended(rounded, (("layer", 1),), 1)
        result = jnp.einsum(
            "kld,lde->kle", rounded, diag_blocks, preferred_element_type=jnp.float32
        )
        result = result + jnp.einsum(
            "kle,lde->kld", padded[:, 2:], couplings, preferred_element_type=jnp.float32
        )
        return result + jnp.einsum(
            "kld,lde->kle", padded[:, :-2], links_below, preferred_element_type=jnp.float32
        )

    def filter_block(start):
        previous = start
        current = (apply_operator(start) - centre * start) / half_width
        for degree_index in range(DEG - 1):
            following = 2.0 * (apply_operator(current) - centre * current) / half_width - previous
            previous = current
            current = following
        return current

    def orthonormal(filtered):
        flat = filtered.reshape(count_vec, layers * width)
        gram = lax.psum(inner_products(flat, flat), "layer") / length_all
        return left_solve(jnp.linalg.cholesky(gram), flat)

    current_block = orthonormal(filter_block(current_block)).reshape(count_vec, layers, width)
    filtered = filter_block(current_block)
    final = orthonormal(filtered)
    low_edge = final[:EDGE]
    high_edge = final[count_vec - EDGE :]
    below_high = shifted(high_edge.astype(jnp.bfloat16), "cuts", 1).astype(high_edge.dtype)
    above_low = shifted(low_edge.astype(jnp.bfloat16), "cuts", -1).astype(low_edge.dtype)
    correlation_low, correlation_high = lax.psum(
        (inner_products(below_high, low_edge), inner_products(above_low, high_edge)), "layer"
    )
    low_new = low_edge - jnp.einsum(
        "wv,wn->vn", correlation_low / length_all, below_high, precision=lax.Precision.HIGHEST
    )
    high_new = high_edge - jnp.einsum(
        "wv,wn->vn", correlation_high / length_all, above_low, precision=lax.Precision.HIGHEST
    )
    result = jnp.concatenate([low_new, final[EDGE : count_vec - EDGE], high_new], 0)
    return result.reshape(1, count_vec, layers, width)


def solution(mesh):
    in_specs = (
        P("cuts", None, "layer", None),
        P("layer", None, None),
        P("layer", None, None),
        P("cuts", None),
    )
    out_specs = P("cuts", None, "layer", None)
    return jax.shard_map(
        per_device, mesh=mesh, in_specs=in_specs, out_specs=out_specs, check_vma=False
    )
```

profile of v0, /device:TPU:138, one launch (start us, length us, event | category | flops | bytes accessed | tf_op | source)
XLA Modules:
  0.0 574.1 jit_solution(272118990598733513)
XLA Ops:
  0.0 2.8 fusion.112
  2.9 2.2 collective-permute-start.1
  5.3 4.3 collective-permute-start.2
  9.6 4.9 collective-permute-start
  18.6 17.0 %collective-permute-done.2 = bf16[64,1,1024]{2,0,1:T(8,128)(2,1)S(1)} collective-permute-done((bf16[64,1,1024]{2,0,1:T(8,128)(2,1)S(1)}, bf16[64,1,1024]{2,0,1:T(8,128)(2,1)S(1)}, u32[]{:S(2)}, u32[]{:S(2)}) %collective-permute-start.2) | collective-permute-done | bytes 131104 | tf_op jit(solution)/shard_map/ppermute | solution.py:21
  36.7 4.5 collective-permute-start.4
  42.0 4.7 collective-permute-start.3
  50.8 2.5 collective-permute-start.6
  54.2 6.8 %collective-permute-start.5 = (bf16[64,1,1024]{2,0,1:T(8,128)(2,1)S(1)}, bf16[64,1,1024]{2,0,1:T(8,128)(2,1)S(1)}, u32[]{:S(2)}, u32[]{:S(2)}) collective-permute-start(bf16[64,1,1024]{2,0,1:T(8,128)(2,1)S(1)} %get-tuple-element.23), channel_id=1, source_target_pairs={{1,0},{2,1},{3,2},{4,3},{5,4},{6,5},{7,6},{8,7},{9,8},{10,9},{11,1... | collective-permute-start | bytes 393224 | tf_op jit(solution)/shard_map/ppermute | solution.py:24
  65.0 1.9 collective-permute-start.8
  67.8 7.4 %collective-permute-start.7 = (bf16[64,1,1024]{2,0,1:T(8,128)(2,1)S(1)}, bf16[64,1,1024]{2,0,1:T(8,128)(2,1)S(1)}, u32[]{:S(2)}, u32[]{:S(2)}) collective-permute-start(bf16[64,1,1024]{2,0,1:T(8,128)(2,1)S(1)} %get-tuple-element.21), channel_id=1, source_target_pairs={{1,0},{2,1},{3,2},{4,3},{5,4},{6,5},{7,6},{8,7},{9,8},{10,9},{11,1... | collective-permute-start | bytes 393224 | tf_op jit(solution)/shard_map/ppermute | solution.py:24
  79.8 134.1 %psum.28 = f32[64,64]{0,1:T(8,128)S(1)} all-reduce(f32[64,64]{0,1:T(8,128)S(1)} %convolution_bitcast_fusion.11), channel_id=1, replica_groups=mesh['cuts'=8,'layer'=32] {'layer'}, use_global_device_ids=true, to_apply=%region_0.0 | all-reduce | flops 4096 | bytes 32768 | tf_op jit(solution)/shard_map/psum | solution.py:72
  214.0 5.8 %cholesky.44 = f32[64,64]{1,0:T(8,128)S(1)} custom-call(f32[64,64]{1,0:T(8,128)S(1)} %fusion.87), custom_call_target="Cholesky" | custom-call | tf_op jit(solution)/shard_map/jit(cholesky)/cholesky | solution.py:73
  221.2 4.9 custom-call.6
  226.9 1.9 collective-permute-start.10
  228.8 3.0 fusion.132
  231.9 7.5 %collective-permute-start.9 = (bf16[64,1,1024]{2,0,1:T(8,128)(2,1)S(1)}, bf16[64,1,1024]{2,0,1:T(8,128)(2,1)S(1)}, u32[]{:S(2)}, u32[]{:S(2)}) collective-permute-start(bf16[64,1,1024]{2,0,1:T(8,128)(2,1)S(1)} %get-tuple-element.19), channel_id=1, source_target_pairs={{1,0},{2,1},{3,2},{4,3},{5,4},{6,5},{7,6},{8,7},{9,8},{10,9},{11,1... | collective-permute-start | bytes 393224 | tf_op jit(solution)/shard_map/ppermute | solution.py:24
  243.3 1.9 collective-permute-start.12
  246.1 7.4 %collective-permute-start.11 = (bf16[64,1,1024]{2,0,1:T(8,128)(2,1)S(1)}, bf16[64,1,1024]{2,0,1:T(8,128)(2,1)S(1)}, u32[]{:S(2)}, u32[]{:S(2)}) collective-permute-start(bf16[64,1,1024]{2,0,1:T(8,128)(2,1)S(1)} %get-tuple-element.17), channel_id=1, source_target_pairs={{1,0},{2,1},{3,2},{4,3},{5,4},{6,5},{7,6},{8,7},{9,8},{10,9},{11,1... | collective-permute-start | bytes 393224 | tf_op jit(solution)/shard_map/ppermute | solution.py:24
  254.4 1.6 collective-permute-done.11
  257.5 1.9 collective-permute-start.14
  260.3 7.4 %collective-permute-start.13 = (bf16[64,1,1024]{2,0,1:T(8,128)(2,1)S(1)}, bf16[64,1,1024]{2,0,1:T(8,128)(2,1)S(1)}, u32[]{:S(2)}, u32[]{:S(2)}) collective-permute-start(bf16[64,1,1024]{2,0,1:T(8,128)(2,1)S(1)} %get-tuple-element.15), channel_id=1, source_target_pairs={{1,0},{2,1},{3,2},{4,3},{5,4},{6,5},{7,6},{8,7},{9,8},{10,9},{11,1... | collective-permute-start | bytes 393224 | tf_op jit(solution)/shard_map/ppermute | solution.py:24
  268.5 1.6 collective-permute-done.13
  271.6 1.9 collective-permute-start.16
  274.4 7.6 %collective-permute-start.15 = (bf16[64,1,1024]{2,0,1:T(8,128)(2,1)S(1)}, bf16[64,1,1024]{2,0,1:T(8,128)(2,1)S(1)}, u32[]{:S(2)}, u32[]{:S(2)}) collective-permute-start(bf16[64,1,1024]{2,0,1:T(8,128)(2,1)S(1)} %get-tuple-element.13), channel_id=1, source_target_pairs={{1,0},{2,1},{3,2},{4,3},{5,4},{6,5},{7,6},{8,7},{9,8},{10,9},{11,1... | collective-permute-start | bytes 393224 | tf_op jit(solution)/shard_map/ppermute | solution.py:24
  286.3 134.0 %psum.29 = f32[64,64]{0,1:T(8,128)S(1)} all-reduce(f32[64,64]{0,1:T(8,128)S(1)} %convolution_bitcast_fusion.10), channel_id=1, replica_groups=mesh['cuts'=8,'layer'=32] {'layer'}, use_global_device_ids=true, to_apply=%region_3.6 | all-reduce | flops 4096 | bytes 32768 | tf_op jit(solution)/shard_map/psum | solution.py:72
  420.4 5.8 %cholesky.55 = f32[64,64]{1,0:T(8,128)S(1)} custom-call(f32[64,64]{1,0:T(8,128)S(1)} %fusion.84), custom_call_target="Cholesky" | custom-call | tf_op jit(solution)/shard_map/jit(cholesky)/cholesky | solution.py:73
  427.6 4.9 custom-call.7
  433.2 3.3 collective-permute-start.17
  436.5 2.6 collective-permute-start.18
  439.6 4.0 collective-permute-done.18
  443.7 128.6 %all-reduce = (f32[16,16]{1,0:T(8,128)S(1)}, f32[16,16]{1,0:T(8,128)S(1)}) all-reduce(f32[16,16]{1,0:T(8,128)S(1)} %fusion.76, f32[16,16]{1,0:T(8,128)S(1)} %fusion.78), channel_id=1, replica_groups=mesh['cuts'=8,'layer'=32] {'layer'}, use_global_device_ids=true, to_apply=%region_5.8 | all-reduce | flops 512 | bytes 4096 | tf_op jit(solution)/shard_map/psum | solution.py:82
  (91 shorter events, 41.2 us)
Async XLA Ops:
  0.0 5.1 copy-start.4
  0.0 14.4 %copy-start = (bf16[2,1024,1024]{2,1,0:T(8,128)(2,1)S(1)}, bf16[2,1024,1024]{2,1,0:T(8,128)(2,1)}, u32[]{:S(2)}) copy-start(bf16[2,1024,1024]{2,1,0:T(8,128)(2,1)} %param.8) | copy-start | bytes 12582916
  2.8 12.5 %copy-start.5 = (s32[1,2]{1,0:T(1,128)S(1)}, s32[1,2]{1,0:T(1,128)}, u32[]{:S(2)}) copy-start(s32[1,2]{1,0:T(1,128)} %param.10) | copy-start | bytes 28
  2.9 14.4 %copy-start.2 = (bf16[2,1024,1024]{2,1,0:T(8,128)(2,1)S(1)}, bf16[2,1024,1024]{2,1,0:T(8,128)(2,1)}, u32[]{:S(2)}) copy-start(bf16[2,1024,1024]{2,1,0:T(8,128)(2,1)} %param.9) | copy-start | bytes 12582916
  2.9 32.7 %collective-permute-start.1 = (bf16[1,1024,1024]{2,1,0:T(8,128)(2,1)S(1)}, bf16[1,1024,1024]{2,1,0:T(8,128)(2,1)S(1)}, u32[]{:S(2)}, u32[]{:S(2)}) collective-permute-start(bf16[1,1024,1024]{2,1,0:T(8,128)(2,1)S(1)} %get-tuple-element.9), channel_id=1, source_target_pairs={{0,1},{1,2},{2,3},{3,4},{4,5},{5,6},{6,7},{7,8},{8,9},{9,10},{10,1... | collective-permute-start | bytes 6291464 | tf_op jit(solution)/shard_map/ppermute | solution.py:13
  5.3 30.3 %collective-permute-start.2 = (bf16[64,1,1024]{2,0,1:T(8,128)(2,1)S(1)}, bf16[64,1,1024]{2,0,1:T(8,128)(2,1)S(1)}, u32[]{:S(2)}, u32[]{:S(2)}) collective-permute-start(bf16[64,1,1024]{2,0,1:T(8,128)(2,1)S(1)} %get-tuple-element.27), channel_id=1, source_target_pairs={{0,1},{1,2},{2,3},{3,4},{4,5},{5,6},{6,7},{7,8},{8,9},{9,10},{10,1... | collective-permute-start | bytes 393224 | tf_op jit(solution)/shard_map/ppermute | solution.py:21
  9.6 7.6 %collective-permute-start = (bf16[64,1,1024]{2,0,1:T(8,128)(2,1)S(1)}, bf16[64,1,1024]{2,0,1:T(8,128)(2,1)S(1)}, u32[]{:S(2)}, u32[]{:S(2)}) collective-permute-start(bf16[64,1,1024]{2,0,1:T(8,128)(2,1)S(1)} %get-tuple-element.28), channel_id=1, source_target_pairs={{1,0},{2,1},{3,2},{4,3},{5,4},{6,5},{7,6},{8,7},{9,8},{10,9},{11,1... | collective-permute-start | bytes 393224 | tf_op jit(solution)/shard_map/ppermute | solution.py:24
  35.6 39.6 %copy-start.6 = (bf16[1,1024,1024]{2,1,0:T(8,128)(2,1)}, bf16[1,1024,1024]{2,1,0:T(8,128)(2,1)S(1)}, u32[]{:S(2)}) copy-start(bf16[1,1024,1024]{2,1,0:T(8,128)(2,1)S(1)} %collective-permute-done.1) | copy-start | bytes 6291460
  36.7 10.1 %collective-permute-start.4 = (bf16[64,1,1024]{2,0,1:T(8,128)(2,1)S(1)}, bf16[64,1,1024]{2,0,1:T(8,128)(2,1)S(1)}, u32[]{:S(2)}, u32[]{:S(2)}) collective-permute-start(bf16[64,1,1024]{2,0,1:T(8,128)(2,1)S(1)} %get-tuple-element.26), channel_id=1, source_target_pairs={{0,1},{1,2},{2,3},{3,4},{4,5},{5,6},{6,7},{7,8},{8,9},{9,10},{10,1... | collective-permute-start | bytes 393224 | tf_op jit(solution)/shard_map/ppermute | solution.py:21
  42.0 7.2 %collective-permute-start.3 = (bf16[64,1,1024]{2,0,1:T(8,128)(2,1)S(1)}, bf16[64,1,1024]{2,0,1:T(8,128)(2,1)S(1)}, u32[]{:S(2)}, u32[]{:S(2)}) collective-permute-start(bf16[64,1,1024]{2,0,1:T(8,128)(2,1)S(1)} %get-tuple-element.25), channel_id=1, source_target_pairs={{1,0},{2,1},{3,2},{4,3},{5,4},{6,5},{7,6},{8,7},{9,8},{10,9},{11,1... | collective-permute-start | bytes 393224 | tf_op jit(solution)/shard_map/ppermute | solution.py:24
  50.8 10.2 %collective-permute-start.6 = (bf16[64,1,1024]{2,0,1:T(8,128)(2,1)S(1)}, bf16[64,1,1024]{2,0,1:T(8,128)(2,1)S(1)}, u32[]{:S(2)}, u32[]{:S(2)}) collective-permute-start(bf16[64,1,1024]{2,0,1:T(8,128)(2,1)S(1)} %get-tuple-element.24), channel_id=1, source_target_pairs={{0,1},{1,2},{2,3},{3,4},{4,5},{5,6},{6,7},{7,8},{8,9},{9,10},{10,1... | collective-permute-start | bytes 393224 | tf_op jit(solution)/shard_map/ppermute | solution.py:21
  54.2 9.3 %collective-permute-start.5 = (bf16[64,1,1024]{2,0,1:T(8,128)(2,1)S(1)}, bf16[64,1,1024]{2,0,1:T(8,128)(2,1)S(1)}, u32[]{:S(2)}, u32[]{:S(2)}) collective-permute-start(bf16[64,1,1024]{2,0,1:T(8,128)(2,1)S(1)} %get-tuple-element.23), channel_id=1, source_target_pairs={{1,0},{2,1},{3,2},{4,3},{5,4},{6,5},{7,6},{8,7},{9,8},{10,9},{11,1... | collective-permute-start | bytes 393224 | tf_op jit(solution)/shard_map/ppermute | solution.py:24
  65.0 10.2 %collective-permute-start.8 = (bf16[64,1,1024]{2,0,1:T(8,128)(2,1)S(1)}, bf16[64,1,1024]{2,0,1:T(8,128)(2,1)S(1)}, u32[]{:S(2)}, u32[]{:S(2)}) collective-permute-start(bf16[64,1,1024]{2,0,1:T(8,128)(2,1)S(1)} %get-tuple-element.22), channel_id=1, source_target_pairs={{0,1},{1,2},{2,3},{3,4},{4,5},{5,6},{6,7},{7,8},{8,9},{9,10},{10,1... | collective-permute-start | bytes 393224 | tf_op jit(solution)/shard_map/ppermute | solution.py:21
  67.8 9.9 %collective-permute-start.7 = (bf16[64,1,1024]{2,0,1:T(8,128)(2,1)S(1)}, bf16[64,1,1024]{2,0,1:T(8,128)(2,1)S(1)}, u32[]{:S(2)}, u32[]{:S(2)}) collective-permute-start(bf16[64,1,1024]{2,0,1:T(8,128)(2,1)S(1)} %get-tuple-element.21), channel_id=1, source_target_pairs={{1,0},{2,1},{3,2},{4,3},{5,4},{6,5},{7,6},{8,7},{9,8},{10,9},{11,1... | collective-permute-start | bytes 393224 | tf_op jit(solution)/shard_map/ppermute | solution.py:24
  226.2 13.2 %copy-start.7 = (bf16[1,1024,1024]{2,1,0:T(8,128)(2,1)S(1)}, bf16[1,1024,1024]{2,1,0:T(8,128)(2,1)}, u32[]{:S(2)}) copy-start(bf16[1,1024,1024]{2,1,0:T(8,128)(2,1)} %copy-done.6) | copy-start | bytes 6291460
  226.9 12.5 %collective-permute-start.10 = (bf16[64,1,1024]{2,0,1:T(8,128)(2,1)S(1)}, bf16[64,1,1024]{2,0,1:T(8,128)(2,1)S(1)}, u32[]{:S(2)}, u32[]{:S(2)}) collective-permute-start(bf16[64,1,1024]{2,0,1:T(8,128)(2,1)S(1)} %get-tuple-element.20), channel_id=1, source_target_pairs={{0,1},{1,2},{2,3},{3,4},{4,5},{5,6},{6,7},{7,8},{8,9},{9,10},{10,1... | collective-permute-start | bytes 393224 | tf_op jit(solution)/shard_map/ppermute | solution.py:21
  231.8 10.0 %copy-start.3 = (bf16[2,1024,1024]{2,1,0:T(8,128)(2,1)S(1)}, bf16[2,1024,1024]{2,1,0:T(8,128)(2,1)}, u32[]{:S(2)}) copy-start(bf16[2,1024,1024]{2,1,0:T(8,128)(2,1)} %param.9) | copy-start | bytes 12582916
  231.9 10.0 %collective-permute-start.9 = (bf16[64,1,1024]{2,0,1:T(8,128)(2,1)S(1)}, bf16[64,1,1024]{2,0,1:T(8,128)(2,1)S(1)}, u32[]{:S(2)}, u32[]{:S(2)}) collective-permute-start(bf16[64,1,1024]{2,0,1:T(8,128)(2,1)S(1)} %get-tuple-element.19), channel_id=1, source_target_pairs={{1,0},{2,1},{3,2},{4,3},{5,4},{6,5},{7,6},{8,7},{9,8},{10,9},{11,1... | collective-permute-start | bytes 393224 | tf_op jit(solution)/shard_map/ppermute | solution.py:24
  240.3 5.0 copy-start.1
  243.3 10.2 %collective-permute-start.12 = (bf16[64,1,1024]{2,0,1:T(8,128)(2,1)S(1)}, bf16[64,1,1024]{2,0,1:T(8,128)(2,1)S(1)}, u32[]{:S(2)}, u32[]{:S(2)}) collective-permute-start(bf16[64,1,1024]{2,0,1:T(8,128)(2,1)S(1)} %get-tuple-element.18), channel_id=1, source_target_pairs={{0,1},{1,2},{2,3},{3,4},{4,5},{5,6},{6,7},{7,8},{8,9},{9,10},{10,1... | collective-permute-start | bytes 393224 | tf_op jit(solution)/shard_map/ppermute | solution.py:21
  246.1 9.9 %collective-permute-start.11 = (bf16[64,1,1024]{2,0,1:T(8,128)(2,1)S(1)}, bf16[64,1,1024]{2,0,1:T(8,128)(2,1)S(1)}, u32[]{:S(2)}, u32[]{:S(2)}) collective-permute-start(bf16[64,1,1024]{2,0,1:T(8,128)(2,1)S(1)} %get-tuple-element.17), channel_id=1, source_target_pairs={{1,0},{2,1},{3,2},{4,3},{5,4},{6,5},{7,6},{8,7},{9,8},{10,9},{11,1... | collective-permute-start | bytes 393224 | tf_op jit(solution)/shard_map/ppermute | solution.py:24
  257.5 10.2 %collective-permute-start.14 = (bf16[64,1,1024]{2,0,1:T(8,128)(2,1)S(1)}, bf16[64,1,1024]{2,0,1:T(8,128)(2,1)S(1)}, u32[]{:S(2)}, u32[]{:S(2)}) collective-permute-start(bf16[64,1,1024]{2,0,1:T(8,128)(2,1)S(1)} %get-tuple-element.16), channel_id=1, source_target_pairs={{0,1},{1,2},{2,3},{3,4},{4,5},{5,6},{6,7},{7,8},{8,9},{9,10},{10,1... | collective-permute-start | bytes 393224 | tf_op jit(solution)/shard_map/ppermute | solution.py:21
  260.3 9.9 %collective-permute-start.13 = (bf16[64,1,1024]{2,0,1:T(8,128)(2,1)S(1)}, bf16[64,1,1024]{2,0,1:T(8,128)(2,1)S(1)}, u32[]{:S(2)}, u32[]{:S(2)}) collective-permute-start(bf16[64,1,1024]{2,0,1:T(8,128)(2,1)S(1)} %get-tuple-element.15), channel_id=1, source_target_pairs={{1,0},{2,1},{3,2},{4,3},{5,4},{6,5},{7,6},{8,7},{9,8},{10,9},{11,1... | collective-permute-start | bytes 393224 | tf_op jit(solution)/shard_map/ppermute | solution.py:24
  271.6 10.4 %collective-permute-start.16 = (bf16[64,1,1024]{2,0,1:T(8,128)(2,1)S(1)}, bf16[64,1,1024]{2,0,1:T(8,128)(2,1)S(1)}, u32[]{:S(2)}, u32[]{:S(2)}) collective-permute-start(bf16[64,1,1024]{2,0,1:T(8,128)(2,1)S(1)} %get-tuple-element.14), channel_id=1, source_target_pairs={{0,1},{1,2},{2,3},{3,4},{4,5},{5,6},{6,7},{7,8},{8,9},{9,10},{10,1... | collective-permute-start | bytes 393224 | tf_op jit(solution)/shard_map/ppermute | solution.py:21
  274.4 9.9 %collective-permute-start.15 = (bf16[64,1,1024]{2,0,1:T(8,128)(2,1)S(1)}, bf16[64,1,1024]{2,0,1:T(8,128)(2,1)S(1)}, u32[]{:S(2)}, u32[]{:S(2)}) collective-permute-start(bf16[64,1,1024]{2,0,1:T(8,128)(2,1)S(1)} %get-tuple-element.13), channel_id=1, source_target_pairs={{1,0},{2,1},{3,2},{4,3},{5,4},{6,5},{7,6},{8,7},{9,8},{10,9},{11,1... | collective-permute-start | bytes 393224 | tf_op jit(solution)/shard_map/ppermute | solution.py:24
  433.2 6.2 %collective-permute-start.17 = (bf16[16,2048]{1,0:T(8,128)(2,1)S(1)}, bf16[16,2048]{1,0:T(8,128)(2,1)S(1)}, u32[]{:S(2)}, u32[]{:S(2)}) collective-permute-start(bf16[16,2048]{1,0:T(8,128)(2,1)S(1)} %get-tuple-element.11), channel_id=1, source_target_pairs={{0,32},{32,64},{64,96},{96,128},{128,160},{160,192},{192,224},{1,3... | collective-permute-start | bytes 196616 | tf_op jit(solution)/shard_map/ppermute | solution.py:13
  436.5 7.1 %collective-permute-start.18 = (bf16[16,2048]{1,0:T(8,128)(2,1)S(1)}, bf16[16,2048]{1,0:T(8,128)(2,1)S(1)}, u32[]{:S(2)}, u32[]{:S(2)}) collective-permute-start(bf16[16,2048]{1,0:T(8,128)(2,1)S(1)} %get-tuple-element.12), channel_id=1, source_target_pairs={{32,0},{64,32},{96,64},{128,96},{160,128},{192,160},{224,192},{33,... | collective-permute-start | bytes 196616 | tf_op jit(solution)/shard_map/ppermute | solution.py:13
where the time goes:
time: 575 us; the launch traced here: 574 us
  blocking collectives  397 us (69%)
  starting transfers between devices  82.6 us (14%)
  waiting for transfers between devices  32.6 us (6%)
  matrix products  30.7 us (5%)
  other arithmetic  24.2 us (4%)
    psum x2, blocking collectives, orthonormal(): gram = lax.psum(inner_products(flat, flat), 'layer') / length_all  268 us
    psum x1, blocking collectives, per_device(): lax.psum((inner_products(below_high, low_edge), inner_products(above_low,...  129 us
    ppermute x8, starting transfers between devices, extended(): lax.ppermute(lax.slice_in_dim(block, 0, width, axis=dim), axis, backward)  53.7 us
    ppermute x8, starting transfers between devices, extended(): lax.ppermute(lax.slice_in_dim(block, block.shape[dim] - width, None, axis...  20.9 us
    ppermute x8, waiting for transfers between devices, extended(): lax.ppermute(lax.slice_in_dim(block, block.shape[dim] - width, None, axis...  17 us
    another operation x6, other arithmetic, orthonormal(): return left_solve(jnp.linalg.cholesky(gram), flat)  13.1 us
    dot_general x8, matrix products, apply_operator(): jnp.einsum('kle,lde->kld', padded[:, 2:], couplings, preferred_element_ty...  11.6 us
  transfers between devices with their start and end apart: 19, of which 10 were waited for; matrix products, arithmetic and copies ran while one was open for 3% of the time, Pallas kernels for 0%

commit v1 on v0

--- a/solution.py
+++ b/solution.py
@@ -5,6 +5,11 @@
 
 EDGE = 16
 DEG = 4
+
+
+def gather_and_add(x, name):
+    shards = lax.all_gather(x, name)
+    return jnp.sum(shards, axis=0)
 
 
 def shifted(block, axis, distance):
@@ -69,7 +74,7 @@
 
     def orthonormal(filtered):
         flat = filtered.reshape(count_vec, layers * width)
-        gram = lax.psum(inner_products(flat, flat), "layer") / length_all
+        gram = gather_and_add(inner_products(flat, flat), "layer") / length_all
         return left_solve(jnp.linalg.cholesky(gram), flat)
 
     current_block = orthonormal(filter_block(current_block)).reshape(count_vec, layers, width)

time: 575 us -> 389 us (0.68)
  blocking collectives: 397 us -> 210 us
    psum x2 -> x0, blocking collectives: 268 us -> none  [orthonormal(): gram = lax.psum(inner_products(flat, flat), 'layer') / length_all]
    all_gather x0 -> x2, blocking collectives: none -> 80.1 us  [gather_and_add(): shards = lax.all_gather(x, name)]
  transfers between devices with their start and end apart: 19 -> 19, of which waited for: 10 -> 10; matrix products, arithmetic and copies ran while one was open for 3% -> 4% of each run, Pallas kernels for 0% -> 0%
where the time goes in v1:
time: 389 us; the launch traced here: 388 us
  blocking collectives  210 us (54%)
  starting transfers between devices  82.7 us (21%)
  waiting for transfers between devices  32.4 us (8%)
  matrix products  30.7 us (8%)
  other arithmetic  24.4 us (6%)
  local copies, waits for them, and re-layouts  5.49 us (1%)
    psum x1, blocking collectives, per_device(): lax.psum((inner_products(below_high, low_edge), inner_products(above_low,...  130 us
    all_gather x2, blocking collectives, gather_and_add(): shards = lax.all_gather(x, name)  80.1 us
    ppermute x8, starting transfers between devices, extended(): lax.ppermute(lax.slice_in_dim(block, 0, width, axis=dim), axis, backward)  52 us
    ppermute x8, starting transfers between devices, extended(): lax.ppermute(lax.slice_in_dim(block, block.shape[dim] - width, None, axis...  22.6 us
    ppermute x8, waiting for transfers between devices, extended(): lax.ppermute(lax.slice_in_dim(block, block.shape[dim] - width, None, axis...  16.8 us
    another operation x6, other arithmetic, orthonormal(): return left_solve(jnp.linalg.cholesky(gram), flat)  13.1 us
    dot_general x8, matrix products, apply_operator(): jnp.einsum('kle,lde->kld', padded[:, 2:], couplings, preferred_element_ty...  11.6 us
    ppermute x8, waiting for transfers between devices, extended(): lax.ppermute(lax.slice_in_dim(block, 0, width, axis=dim), axis, backward)  11.2 us
  transfers between devices with their start and end apart: 19, of which 10 were waited for; matrix products, arithmetic and copies ran while one was open for 4% of the time, Pallas kernels for 0%

profile of v1, /device:TPU:138, one launch (start us, length us, event | category | flops | bytes accessed | tf_op | source)
XLA Modules:
  0.0 387.9 jit_solution(13082902717463475343)
XLA Ops:
  0.0 2.8 fusion.112
  2.9 2.3 collective-permute-start.1
  5.4 4.2 %collective-permute-start.2 = (bf16[64,1,1024]{2,0,1:T(8,128)(2,1)S(1)}, bf16[64,1,1024]{2,0,1:T(8,128)(2,1)S(1)}, u32[]{:S(2)}, u32[]{:S(2)}) collective-permute-start(bf16[64,1,1024]{2,0,1:T(8,128)(2,1)S(1)} %get-tuple-element.27), channel_id=1, source_target_pairs={{0,1},{1,2},{2,3},{3,4},{4,5},{5,6},{6,7},{7,8},{8,9},{9,10},{10,1... | collective-permute-start | bytes 393224 | tf_op jit(solution)/shard_map/ppermute | solution.py:26
  9.6 5.0 %collective-permute-start = (bf16[64,1,1024]{2,0,1:T(8,128)(2,1)S(1)}, bf16[64,1,1024]{2,0,1:T(8,128)(2,1)S(1)}, u32[]{:S(2)}, u32[]{:S(2)}) collective-permute-start(bf16[64,1,1024]{2,0,1:T(8,128)(2,1)S(1)} %get-tuple-element.28), channel_id=1, source_target_pairs={{1,0},{2,1},{3,2},{4,3},{5,4},{6,5},{7,6},{8,7},{9,8},{10,9},{11,1... | collective-permute-start | bytes 393224 | tf_op jit(solution)/shard_map/ppermute | solution.py:29
  18.8 16.8 %collective-permute-done.2 = bf16[64,1,1024]{2,0,1:T(8,128)(2,1)S(1)} collective-permute-done((bf16[64,1,1024]{2,0,1:T(8,128)(2,1)S(1)}, bf16[64,1,1024]{2,0,1:T(8,128)(2,1)S(1)}, u32[]{:S(2)}, u32[]{:S(2)}) %collective-permute-start.2) | collective-permute-done | bytes 131104 | tf_op jit(solution)/shard_map/ppermute | solution.py:26
  36.7 4.5 %collective-permute-start.4 = (bf16[64,1,1024]{2,0,1:T(8,128)(2,1)S(1)}, bf16[64,1,1024]{2,0,1:T(8,128)(2,1)S(1)}, u32[]{:S(2)}, u32[]{:S(2)}) collective-permute-start(bf16[64,1,1024]{2,0,1:T(8,128)(2,1)S(1)} %get-tuple-element.26), channel_id=1, source_target_pairs={{0,1},{1,2},{2,3},{3,4},{4,5},{5,6},{6,7},{7,8},{8,9},{9,10},{10,1... | collective-permute-start | bytes 393224 | tf_op jit(solution)/shard_map/ppermute | solution.py:26
  42.0 4.7 %collective-permute-start.3 = (bf16[64,1,1024]{2,0,1:T(8,128)(2,1)S(1)}, bf16[64,1,1024]{2,0,1:T(8,128)(2,1)S(1)}, u32[]{:S(2)}, u32[]{:S(2)}) collective-permute-start(bf16[64,1,1024]{2,0,1:T(8,128)(2,1)S(1)} %get-tuple-element.25), channel_id=1, source_target_pairs={{1,0},{2,1},{3,2},{4,3},{5,4},{6,5},{7,6},{8,7},{9,8},{10,9},{11,1... | collective-permute-start | bytes 393224 | tf_op jit(solution)/shard_map/ppermute | solution.py:29
  50.8 2.5 collective-permute-start.6
  54.2 6.8 %collective-permute-start.5 = (bf16[64,1,1024]{2,0,1:T(8,128)(2,1)S(1)}, bf16[64,1,1024]{2,0,1:T(8,128)(2,1)S(1)}, u32[]{:S(2)}, u32[]{:S(2)}) collective-permute-start(bf16[64,1,1024]{2,0,1:T(8,128)(2,1)S(1)} %get-tuple-element.23), channel_id=1, source_target_pairs={{1,0},{2,1},{3,2},{4,3},{5,4},{6,5},{7,6},{8,7},{9,8},{10,9},{11,1... | collective-permute-start | bytes 393224 | tf_op jit(solution)/shard_map/ppermute | solution.py:29
  65.0 1.9 collective-permute-start.8
  67.8 7.4 %collective-permute-start.7 = (bf16[64,1,1024]{2,0,1:T(8,128)(2,1)S(1)}, bf16[64,1,1024]{2,0,1:T(8,128)(2,1)S(1)}, u32[]{:S(2)}, u32[]{:S(2)}) collective-permute-start(bf16[64,1,1024]{2,0,1:T(8,128)(2,1)S(1)} %get-tuple-element.21), channel_id=1, source_target_pairs={{1,0},{2,1},{3,2},{4,3},{5,4},{6,5},{7,6},{8,7},{9,8},{10,9},{11,1... | collective-permute-start | bytes 393224 | tf_op jit(solution)/shard_map/ppermute | solution.py:29
  79.8 40.2 %all-gather = f32[2048,64]{1,0:T(8,128)S(1)} all-gather(f32[64,64]{1,0:T(8,128)S(1)} %convolution_bitcast_fusion.11), channel_id=2, replica_groups=mesh['cuts'=8,'layer'=32] {'layer'}, dimensions={0}, use_global_device_ids=true | all-gather | bytes 540672 | tf_op jit(solution)/shard_map/all_gather | solution.py:11
  120.2 5.8 %cholesky.44 = f32[64,64]{1,0:T(8,128)S(1)} custom-call(f32[64,64]{1,0:T(8,128)S(1)} %fusion.87), custom_call_target="Cholesky" | custom-call | tf_op jit(solution)/shard_map/jit(cholesky)/cholesky | solution.py:78
  127.5 4.9 %custom-call.6 = f32[1,64,64]{1,2,0:T(8,128)S(1)} custom-call(f32[1,64,64]{2,1,0:T(8,128)S(1)} %fusion.80), custom_call_target="InvertDiagBlocksLowerTriangular" | custom-call | tf_op jit(solution)/shard_map/triangular_solve/custom-call.0 | solution.py:39
  133.1 2.3 collective-permute-start.10
  135.3 3.0 fusion.132
  138.4 7.2 %collective-permute-start.9 = (bf16[64,1,1024]{2,0,1:T(8,128)(2,1)S(1)}, bf16[64,1,1024]{2,0,1:T(8,128)(2,1)S(1)}, u32[]{:S(2)}, u32[]{:S(2)}) collective-permute-start(bf16[64,1,1024]{2,0,1:T(8,128)(2,1)S(1)} %get-tuple-element.19), channel_id=1, source_target_pairs={{1,0},{2,1},{3,2},{4,3},{5,4},{6,5},{7,6},{8,7},{9,8},{10,9},{11,1... | collective-permute-start | bytes 393224 | tf_op jit(solution)/shard_map/ppermute | solution.py:29
  149.5 3.5 collective-permute-start.12
  153.9 5.8 %collective-permute-start.11 = (bf16[64,1,1024]{2,0,1:T(8,128)(2,1)S(1)}, bf16[64,1,1024]{2,0,1:T(8,128)(2,1)S(1)}, u32[]{:S(2)}, u32[]{:S(2)}) collective-permute-start(bf16[64,1,1024]{2,0,1:T(8,128)(2,1)S(1)} %get-tuple-element.17), channel_id=1, source_target_pairs={{1,0},{2,1},{3,2},{4,3},{5,4},{6,5},{7,6},{8,7},{9,8},{10,9},{11,1... | collective-permute-start | bytes 393224 | tf_op jit(solution)/shard_map/ppermute | solution.py:29
  160.6 1.6 collective-permute-done.11
  163.7 1.9 collective-permute-start.14
  166.5 7.4 %collective-permute-start.13 = (bf16[64,1,1024]{2,0,1:T(8,128)(2,1)S(1)}, bf16[64,1,1024]{2,0,1:T(8,128)(2,1)S(1)}, u32[]{:S(2)}, u32[]{:S(2)}) collective-permute-start(bf16[64,1,1024]{2,0,1:T(8,128)(2,1)S(1)} %get-tuple-element.15), channel_id=1, source_target_pairs={{1,0},{2,1},{3,2},{4,3},{5,4},{6,5},{7,6},{8,7},{9,8},{10,9},{11,1... | collective-permute-start | bytes 393224 | tf_op jit(solution)/shard_map/ppermute | solution.py:29
  174.7 1.6 collective-permute-done.13
  177.8 1.9 collective-permute-start.16
  180.6 7.6 %collective-permute-start.15 = (bf16[64,1,1024]{2,0,1:T(8,128)(2,1)S(1)}, bf16[64,1,1024]{2,0,1:T(8,128)(2,1)S(1)}, u32[]{:S(2)}, u32[]{:S(2)}) collective-permute-start(bf16[64,1,1024]{2,0,1:T(8,128)(2,1)S(1)} %get-tuple-element.13), channel_id=1, source_target_pairs={{1,0},{2,1},{3,2},{4,3},{5,4},{6,5},{7,6},{8,7},{9,8},{10,9},{11,1... | collective-permute-start | bytes 393224 | tf_op jit(solution)/shard_map/ppermute | solution.py:29
  192.6 40.0 %all-gather.1 = f32[2048,64]{1,0:T(8,128)S(1)} all-gather(f32[64,64]{1,0:T(8,128)S(1)} %convolution_bitcast_fusion.10), channel_id=3, replica_groups=mesh['cuts'=8,'layer'=32] {'layer'}, dimensions={0}, use_global_device_ids=true | all-gather | bytes 540672 | tf_op jit(solution)/shard_map/all_gather | solution.py:11
  232.8 5.8 %cholesky.55 = f32[64,64]{1,0:T(8,128)S(1)} custom-call(f32[64,64]{1,0:T(8,128)S(1)} %fusion.84), custom_call_target="Cholesky" | custom-call | tf_op jit(solution)/shard_map/jit(cholesky)/cholesky | solution.py:78
  240.0 4.9 %custom-call.7 = f32[1,64,64]{1,2,0:T(8,128)S(1)} custom-call(f32[1,64,64]{2,1,0:T(8,128)S(1)} %fusion.81), custom_call_target="InvertDiagBlocksLowerTriangular" | custom-call | tf_op jit(solution)/shard_map/triangular_solve/custom-call.0 | solution.py:39
  245.6 3.3 collective-permute-start.17
  248.9 2.6 collective-permute-start.18
  252.0 4.0 %collective-permute-done.18 = bf16[16,2048]{1,0:T(8,128)(2,1)S(1)} collective-permute-done((bf16[16,2048]{1,0:T(8,128)(2,1)S(1)}, bf16[16,2048]{1,0:T(8,128)(2,1)S(1)}, u32[]{:S(2)}, u32[]{:S(2)}) %collective-permute-start.18) | collective-permute-done | bytes 65568 | tf_op jit(solution)/shard_map/ppermute | solution.py:18
  256.1 130.0 %all-reduce = (f32[16,16]{1,0:T(8,128)S(1)}, f32[16,16]{1,0:T(8,128)S(1)}) all-reduce(f32[16,16]{1,0:T(8,128)S(1)} %fusion.76, f32[16,16]{1,0:T(8,128)S(1)} %fusion.78), channel_id=1, replica_groups=mesh['cuts'=8,'layer'=32] {'layer'}, use_global_device_ids=true, to_apply=%region_5.8 | all-reduce | flops 512 | bytes 4096 | tf_op jit(solution)/shard_map/psum | solution.py:87
  (99 shorter events, 41.6 us)
Async XLA Ops:
  0.0 5.2 %copy-start.4 = (f32[1,64,2,1024]{3,2,1,0:T(2,128)S(1)}, f32[1,64,2,1024]{3,2,1,0:T(2,128)}, u32[]{:S(2)}) copy-start(f32[1,64,2,1024]{3,2,1,0:T(2,128)} %param.7) | copy-start | bytes 1572868
  0.0 14.6 %copy-start = (bf16[2,1024,1024]{2,1,0:T(8,128)(2,1)S(1)}, bf16[2,1024,1024]{2,1,0:T(8,128)(2,1)}, u32[]{:S(2)}) copy-start(bf16[2,1024,1024]{2,1,0:T(8,128)(2,1)} %param.8) | copy-start | bytes 12582916
  2.8 72.4 %copy-start.5 = (bf16[1,1024,1024]{2,1,0:T(8,128)(2,1)}, bf16[1,1024,1024]{2,1,0:T(8,128)(2,1)S(1)}, u32[]{:S(2)}) copy-start(bf16[1,1024,1024]{2,1,0:T(8,128)(2,1)S(1)} %get-tuple-element.10) | copy-start | bytes 6291460
  2.9 12.6 %copy-start.7 = (s32[1,2]{1,0:T(1,128)S(1)}, s32[1,2]{1,0:T(1,128)}, u32[]{:S(2)}) copy-start(s32[1,2]{1,0:T(1,128)} %param.10) | copy-start | bytes 28
  2.9 14.5 %copy-start.2 = (bf16[2,1024,1024]{2,1,0:T(8,128)(2,1)S(1)}, bf16[2,1024,1024]{2,1,0:T(8,128)(2,1)}, u32[]{:S(2)}) copy-start(bf16[2,1024,1024]{2,1,0:T(8,128)(2,1)} %param.9) | copy-start | bytes 12582916
  2.9 32.7 %collective-permute-start.1 = (bf16[1,1024,1024]{2,1,0:T(8,128)(2,1)S(1)}, bf16[1,1024,1024]{2,1,0:T(8,128)(2,1)S(1)}, u32[]{:S(2)}, u32[]{:S(2)}) collective-permute-start(bf16[1,1024,1024]{2,1,0:T(8,128)(2,1)S(1)} %get-tuple-element.9), channel_id=1, source_target_pairs={{0,1},{1,2},{2,3},{3,4},{4,5},{5,6},{6,7},{7,8},{8,9},{9,10},{10,1... | collective-permute-start | bytes 6291464 | tf_op jit(solution)/shard_map/ppermute | solution.py:18
  5.4 30.2 %collective-permute-start.2 = (bf16[64,1,1024]{2,0,1:T(8,128)(2,1)S(1)}, bf16[64,1,1024]{2,0,1:T(8,128)(2,1)S(1)}, u32[]{:S(2)}, u32[]{:S(2)}) collective-permute-start(bf16[64,1,1024]{2,0,1:T(8,128)(2,1)S(1)} %get-tuple-element.27), channel_id=1, source_target_pairs={{0,1},{1,2},{2,3},{3,4},{4,5},{5,6},{6,7},{7,8},{8,9},{9,10},{10,1... | collective-permute-start | bytes 393224 | tf_op jit(solution)/shard_map/ppermute | solution.py:26
  9.6 7.8 %collective-permute-start = (bf16[64,1,1024]{2,0,1:T(8,128)(2,1)S(1)}, bf16[64,1,1024]{2,0,1:T(8,128)(2,1)S(1)}, u32[]{:S(2)}, u32[]{:S(2)}) collective-permute-start(bf16[64,1,1024]{2,0,1:T(8,128)(2,1)S(1)} %get-tuple-element.28), channel_id=1, source_target_pairs={{1,0},{2,1},{3,2},{4,3},{5,4},{6,5},{7,6},{8,7},{9,8},{10,9},{11,1... | collective-permute-start | bytes 393224 | tf_op jit(solution)/shard_map/ppermute | solution.py:29
  35.6 39.6 %copy-start.8 = (bf16[1,1024,1024]{2,1,0:T(8,128)(2,1)}, bf16[1,1024,1024]{2,1,0:T(8,128)(2,1)S(1)}, u32[]{:S(2)}) copy-start(bf16[1,1024,1024]{2,1,0:T(8,128)(2,1)S(1)} %collective-permute-done.1) | copy-start | bytes 6291460
  36.7 10.0 %collective-permute-start.4 = (bf16[64,1,1024]{2,0,1:T(8,128)(2,1)S(1)}, bf16[64,1,1024]{2,0,1:T(8,128)(2,1)S(1)}, u32[]{:S(2)}, u32[]{:S(2)}) collective-permute-start(bf16[64,1,1024]{2,0,1:T(8,128)(2,1)S(1)} %get-tuple-element.26), channel_id=1, source_target_pairs={{0,1},{1,2},{2,3},{3,4},{4,5},{5,6},{6,7},{7,8},{8,9},{9,10},{10,1... | collective-permute-start | bytes 393224 | tf_op jit(solution)/shard_map/ppermute | solution.py:26
  42.0 7.2 %collective-permute-start.3 = (bf16[64,1,1024]{2,0,1:T(8,128)(2,1)S(1)}, bf16[64,1,1024]{2,0,1:T(8,128)(2,1)S(1)}, u32[]{:S(2)}, u32[]{:S(2)}) collective-permute-start(bf16[64,1,1024]{2,0,1:T(8,128)(2,1)S(1)} %get-tuple-element.25), channel_id=1, source_target_pairs={{1,0},{2,1},{3,2},{4,3},{5,4},{6,5},{7,6},{8,7},{9,8},{10,9},{11,1... | collective-permute-start | bytes 393224 | tf_op jit(solution)/shard_map/ppermute | solution.py:29
  50.8 10.2 %collective-permute-start.6 = (bf16[64,1,1024]{2,0,1:T(8,128)(2,1)S(1)}, bf16[64,1,1024]{2,0,1:T(8,128)(2,1)S(1)}, u32[]{:S(2)}, u32[]{:S(2)}) collective-permute-start(bf16[64,1,1024]{2,0,1:T(8,128)(2,1)S(1)} %get-tuple-element.24), channel_id=1, source_target_pairs={{0,1},{1,2},{2,3},{3,4},{4,5},{5,6},{6,7},{7,8},{8,9},{9,10},{10,1... | collective-permute-start | bytes 393224 | tf_op jit(solution)/shard_map/ppermute | solution.py:26
  54.2 9.3 %collective-permute-start.5 = (bf16[64,1,1024]{2,0,1:T(8,128)(2,1)S(1)}, bf16[64,1,1024]{2,0,1:T(8,128)(2,1)S(1)}, u32[]{:S(2)}, u32[]{:S(2)}) collective-permute-start(bf16[64,1,1024]{2,0,1:T(8,128)(2,1)S(1)} %get-tuple-element.23), channel_id=1, source_target_pairs={{1,0},{2,1},{3,2},{4,3},{5,4},{6,5},{7,6},{8,7},{9,8},{10,9},{11,1... | collective-permute-start | bytes 393224 | tf_op jit(solution)/shard_map/ppermute | solution.py:29
  65.0 10.2 %collective-permute-start.8 = (bf16[64,1,1024]{2,0,1:T(8,128)(2,1)S(1)}, bf16[64,1,1024]{2,0,1:T(8,128)(2,1)S(1)}, u32[]{:S(2)}, u32[]{:S(2)}) collective-permute-start(bf16[64,1,1024]{2,0,1:T(8,128)(2,1)S(1)} %get-tuple-element.22), channel_id=1, source_target_pairs={{0,1},{1,2},{2,3},{3,4},{4,5},{5,6},{6,7},{7,8},{8,9},{9,10},{10,1... | collective-permute-start | bytes 393224 | tf_op jit(solution)/shard_map/ppermute | solution.py:26
  67.8 9.9 %collective-permute-start.7 = (bf16[64,1,1024]{2,0,1:T(8,128)(2,1)S(1)}, bf16[64,1,1024]{2,0,1:T(8,128)(2,1)S(1)}, u32[]{:S(2)}, u32[]{:S(2)}) collective-permute-start(bf16[64,1,1024]{2,0,1:T(8,128)(2,1)S(1)} %get-tuple-element.21), channel_id=1, source_target_pairs={{1,0},{2,1},{3,2},{4,3},{5,4},{6,5},{7,6},{8,7},{9,8},{10,9},{11,1... | collective-permute-start | bytes 393224 | tf_op jit(solution)/shard_map/ppermute | solution.py:29
  120.2 25.4 %copy-start.6 = (bf16[1,1024,1024]{2,1,0:T(8,128)(2,1)S(1)}, bf16[1,1024,1024]{2,1,0:T(8,128)(2,1)}, u32[]{:S(2)}) copy-start(bf16[1,1024,1024]{2,1,0:T(8,128)(2,1)} %copy-done.5) | copy-start | bytes 6291460
  132.4 13.2 %copy-start.9 = (bf16[1,1024,1024]{2,1,0:T(8,128)(2,1)S(1)}, bf16[1,1024,1024]{2,1,0:T(8,128)(2,1)}, u32[]{:S(2)}) copy-start(bf16[1,1024,1024]{2,1,0:T(8,128)(2,1)} %copy-done.8) | copy-start | bytes 6291460
  133.1 12.5 %collective-permute-start.10 = (bf16[64,1,1024]{2,0,1:T(8,128)(2,1)S(1)}, bf16[64,1,1024]{2,0,1:T(8,128)(2,1)S(1)}, u32[]{:S(2)}, u32[]{:S(2)}) collective-permute-start(bf16[64,1,1024]{2,0,1:T(8,128)(2,1)S(1)} %get-tuple-element.20), channel_id=1, source_target_pairs={{0,1},{1,2},{2,3},{3,4},{4,5},{5,6},{6,7},{7,8},{8,9},{9,10},{10,1... | collective-permute-start | bytes 393224 | tf_op jit(solution)/shard_map/ppermute | solution.py:26
  138.4 9.7 %copy-start.3 = (bf16[2,1024,1024]{2,1,0:T(8,128)(2,1)S(1)}, bf16[2,1024,1024]{2,1,0:T(8,128)(2,1)}, u32[]{:S(2)}) copy-start(bf16[2,1024,1024]{2,1,0:T(8,128)(2,1)} %param.9) | copy-start | bytes 12582916
  138.4 9.7 %collective-permute-start.9 = (bf16[64,1,1024]{2,0,1:T(8,128)(2,1)S(1)}, bf16[64,1,1024]{2,0,1:T(8,128)(2,1)S(1)}, u32[]{:S(2)}, u32[]{:S(2)}) collective-permute-start(bf16[64,1,1024]{2,0,1:T(8,128)(2,1)S(1)} %get-tuple-element.19), channel_id=1, source_target_pairs={{1,0},{2,1},{3,2},{4,3},{5,4},{6,5},{7,6},{8,7},{9,8},{10,9},{11,1... | collective-permute-start | bytes 393224 | tf_op jit(solution)/shard_map/ppermute | solution.py:29
  146.5 6.6 %copy-start.1 = (bf16[2,1024,1024]{2,1,0:T(8,128)(2,1)S(1)}, bf16[2,1024,1024]{2,1,0:T(8,128)(2,1)}, u32[]{:S(2)}) copy-start(bf16[2,1024,1024]{2,1,0:T(8,128)(2,1)} %param.8) | copy-start | bytes 12582916
  149.5 10.2 %collective-permute-start.12 = (bf16[64,1,1024]{2,0,1:T(8,128)(2,1)S(1)}, bf16[64,1,1024]{2,0,1:T(8,128)(2,1)S(1)}, u32[]{:S(2)}, u32[]{:S(2)}) collective-permute-start(bf16[64,1,1024]{2,0,1:T(8,128)(2,1)S(1)} %get-tuple-element.18), channel_id=1, source_target_pairs={{0,1},{1,2},{2,3},{3,4},{4,5},{5,6},{6,7},{7,8},{8,9},{9,10},{10,1... | collective-permute-start | bytes 393224 | tf_op jit(solution)/shard_map/ppermute | solution.py:26
  153.9 8.3 %collective-permute-start.11 = (bf16[64,1,1024]{2,0,1:T(8,128)(2,1)S(1)}, bf16[64,1,1024]{2,0,1:T(8,128)(2,1)S(1)}, u32[]{:S(2)}, u32[]{:S(2)}) collective-permute-start(bf16[64,1,1024]{2,0,1:T(8,128)(2,1)S(1)} %get-tuple-element.17), channel_id=1, source_target_pairs={{1,0},{2,1},{3,2},{4,3},{5,4},{6,5},{7,6},{8,7},{9,8},{10,9},{11,1... | collective-permute-start | bytes 393224 | tf_op jit(solution)/shard_map/ppermute | solution.py:29
  163.7 10.2 %collective-permute-start.14 = (bf16[64,1,1024]{2,0,1:T(8,128)(2,1)S(1)}, bf16[64,1,1024]{2,0,1:T(8,128)(2,1)S(1)}, u32[]{:S(2)}, u32[]{:S(2)}) collective-permute-start(bf16[64,1,1024]{2,0,1:T(8,128)(2,1)S(1)} %get-tuple-element.16), channel_id=1, source_target_pairs={{0,1},{1,2},{2,3},{3,4},{4,5},{5,6},{6,7},{7,8},{8,9},{9,10},{10,1... | collective-permute-start | bytes 393224 | tf_op jit(solution)/shard_map/ppermute | solution.py:26
  166.5 9.9 %collective-permute-start.13 = (bf16[64,1,1024]{2,0,1:T(8,128)(2,1)S(1)}, bf16[64,1,1024]{2,0,1:T(8,128)(2,1)S(1)}, u32[]{:S(2)}, u32[]{:S(2)}) collective-permute-start(bf16[64,1,1024]{2,0,1:T(8,128)(2,1)S(1)} %get-tuple-element.15), channel_id=1, source_target_pairs={{1,0},{2,1},{3,2},{4,3},{5,4},{6,5},{7,6},{8,7},{9,8},{10,9},{11,1... | collective-permute-start | bytes 393224 | tf_op jit(solution)/shard_map/ppermute | solution.py:29
  177.8 10.4 %collective-permute-start.16 = (bf16[64,1,1024]{2,0,1:T(8,128)(2,1)S(1)}, bf16[64,1,1024]{2,0,1:T(8,128)(2,1)S(1)}, u32[]{:S(2)}, u32[]{:S(2)}) collective-permute-start(bf16[64,1,1024]{2,0,1:T(8,128)(2,1)S(1)} %get-tuple-element.14), channel_id=1, source_target_pairs={{0,1},{1,2},{2,3},{3,4},{4,5},{5,6},{6,7},{7,8},{8,9},{9,10},{10,1... | collective-permute-start | bytes 393224 | tf_op jit(solution)/shard_map/ppermute | solution.py:26
  180.6 9.9 %collective-permute-start.15 = (bf16[64,1,1024]{2,0,1:T(8,128)(2,1)S(1)}, bf16[64,1,1024]{2,0,1:T(8,128)(2,1)S(1)}, u32[]{:S(2)}, u32[]{:S(2)}) collective-permute-start(bf16[64,1,1024]{2,0,1:T(8,128)(2,1)S(1)} %get-tuple-element.13), channel_id=1, source_target_pairs={{1,0},{2,1},{3,2},{4,3},{5,4},{6,5},{7,6},{8,7},{9,8},{10,9},{11,1... | collective-permute-start | bytes 393224 | tf_op jit(solution)/shard_map/ppermute | solution.py:29
  245.6 6.2 %collective-permute-start.17 = (bf16[16,2048]{1,0:T(8,128)(2,1)S(1)}, bf16[16,2048]{1,0:T(8,128)(2,1)S(1)}, u32[]{:S(2)}, u32[]{:S(2)}) collective-permute-start(bf16[16,2048]{1,0:T(8,128)(2,1)S(1)} %get-tuple-element.11), channel_id=1, source_target_pairs={{0,32},{32,64},{64,96},{96,128},{128,160},{160,192},{192,224},{1,3... | collective-permute-start | bytes 196616 | tf_op jit(solution)/shard_map/ppermute | solution.py:18
  248.9 7.1 %collective-permute-start.18 = (bf16[16,2048]{1,0:T(8,128)(2,1)S(1)}, bf16[16,2048]{1,0:T(8,128)(2,1)S(1)}, u32[]{:S(2)}, u32[]{:S(2)}) collective-permute-start(bf16[16,2048]{1,0:T(8,128)(2,1)S(1)} %get-tuple-element.12), channel_id=1, source_target_pairs={{32,0},{64,32},{96,64},{128,96},{160,128},{192,160},{224,192},{33,... | collective-permute-start | bytes 196616 | tf_op jit(solution)/shard_map/ppermute | solution.py:18
